TPU v7x, 256 devices: a whole 4x4x8 slice. The times are simulated.
256 devices in a mesh: seq: 16 (over z, x_lo), wr: 4 (over y), wc: 4 (over x_hi, core).
Axes of the slice: x: 4 (x_hi: 2, x_lo: 2; x = x_hi * 2 + x_lo), y: 4, z: 8, core: 2. Of those that a mesh axis runs over, the one named last changes fastest.
Arguments:
- tokens: bfloat16 [8192, 2048], P('seq', ('wr', 'wc')), may hold values from -6 to 6
- ln_gain: float32 [2, 2048], replicated, may hold values from 0.5 to 1.5
- w_branch: bfloat16 [2, 2048, 4096], P(None, None, ('wr', 'wc')), may hold values from -0.125 to 0.125
- w_outgate: bfloat16 [2, 2048, 4096], P(None, None, ('wr', 'wc')), may hold values from -0.125 to 0.125
- w_gates: bfloat16 [2, 2048, 8], replicated, may hold values from -0.125 to 0.125
- forget_bias: float32 [2, 4], replicated, may hold values from 3.2 to 11
- conv_weight: float32 [2, 4, 4096], P(None, None, ('wr', 'wc')), may hold values from -3 to 3
- conv_bias: float32 [2, 4096], P(None, ('wr', 'wc')), may hold values from -3 to 3
- w_query: float32 [2, 4, 4, 4, 256], P(None, 'wr'), may hold values from -3 to 3
- w_key: float32 [2, 4, 4, 4, 256], P(None, 'wr'), may hold values from -3 to 3
- w_value: float32 [2, 4, 4, 4, 256], P(None, 'wr', None, 'wc'), may hold values from -4 to 4
- skip_gain: float32 [2, 4096], P(None, ('wr', 'wc')), may hold values from 0.5 to 1.5
- norm_gain: float32 [2, 4096], P(None, ('wr', 'wc')), may hold values from 0.5 to 1.5
- w_down: bfloat16 [2, 4096, 2048], P(None, ('wr', 'wc')), may hold values from -0.125 to 0.125
- lengths: int32 [3], replicated, may hold values from 1 to 4096, 8192 in all
- request_prompt: int32 [32], P('seq'), may hold values from 0 to 2
Outputs:
- mixed: bfloat16 [8192, 2048], P('seq', ('wr', 'wc'))
- request_state: bfloat16 [2, 32, 4, 1024, 1024], P(None, 'seq', 'wr', None, 'wc')
- request_conv: bfloat16 [2, 32, 3, 4096], P(None, 'seq', None, ('wr', 'wc'))
Inputs may be any that keep to these rules, and one draw needn't show every extreme that they name: `lengths`: the 3 prompts lie end to end in order and fill all 8192 positions; the longest has exactly 4096 positions.
All inputs are finite; a program needn't handle non-finite values.
Results may differ from a plain program's by a relative error of at most 0.035.
Values may be sent and summed in bfloat16 or wider, within the bound.
A program may use at most 128 MiB of HBM per device.

v0:
```python
import jax
import jax.numpy as jnp
from jax import lax
from jax.sharding import PartitionSpec as P

HEADS = 4
CONV = 4
LAYERS = 2
PROMPTS = 3


EPSILON = 1e-05
GATE_CAP = 15.0
ROW_DIMS = (((0,), (0,)), ((), ()))
FEATURE_DIMS = (((1,), (1,)), ((), ()))


def shifted(value, axis, steps):
    count = lax.axis_size(axis)
    first, last = (max(0, -steps), min(count, count - steps))
    return lax.ppermute(value, axis, [(source, source + steps) for source in range(first, last)])


def entering_2(shard, axis, join, neutral):
    place = lax.axis_index(axis)
    gathered = jax.tree.map(
        lambda a, kind: lax.all_gather(a.astype(kind), axis), shard, (jnp.bfloat16, jnp.bfloat16)
    )
    state = jax.tree.map(lambda a, e: jnp.zeros_like(a) + jnp.asarray(e, a.dtype), shard, neutral)

    def one(step, state):
        return join(
            state,
            jax.tree.map(
                lambda a, own: lax.dynamic_index_in_dim(a, step, 0, False).astype(own.dtype),
                gathered,
                shard,
            ),
        )

    return lax.fori_loop(0, place, one, state)


def broadcast(shard, axis, root):
    mine = lax.axis_index(axis) == root
    return lax.psum(jnp.where(mine, shard, jnp.zeros_like(shard)), axis)


def norm_rows(source, gain_row):
    widened = source.astype(jnp.float32)
    row_mean = jnp.mean(widened, axis=1, keepdims=True)
    row_var = jnp.mean(widened * widened, axis=1, keepdims=True) - row_mean * row_mean
    return ((widened - row_mean) * lax.rsqrt(row_var + EPSILON) * gain_row).astype(jnp.bfloat16)


def segment_of(positions, lengths):
    bound_one = lengths[0]
    bound_two = lengths[0] + lengths[1]
    return (positions >= bound_one).astype(jnp.int32) + (positions >= bound_two).astype(jnp.int32)


def conv_rows(extended, ext_segment, segment, weight, bias_row):
    row_count = segment.shape[0]
    widened = extended.astype(jnp.float32)
    summed = jnp.zeros((row_count, widened.shape[1]), jnp.float32) + bias_row
    for back_step in range(weight.shape[0]):
        low_row = weight.shape[0] - 1 - back_step
        keep_row = (ext_segment[low_row : low_row + row_count] == segment).astype(jnp.float32)
        summed = (
            summed + weight[back_step] * widened[low_row : low_row + row_count] * keep_row[:, None]
        )
    return jax.nn.silu(summed).astype(jnp.bfloat16)


def block_mix(source, weight):
    row_count = source.shape[0]
    grouped = source.astype(jnp.float32).reshape(row_count, 4, -1)
    mixed = jnp.einsum("tig,ijg->tjg", grouped, weight, precision=lax.Precision.HIGHEST)
    return mixed.reshape(row_count, -1)


def block_terms(queries, key_rows, values, log_forget, in_gate, segment, prev_seg):
    row_count = queries.shape[0]
    cum_log = jnp.cumsum(log_forget)
    row_order = jnp.arange(row_count)
    allowed = (row_order[:, None] >= row_order[None, :]) & (segment[:, None] == segment[None, :])
    exponent = jnp.where(allowed, cum_log[:, None] - cum_log[None, :] + in_gate[None, :], -jnp.inf)
    scores = lax.dot_general(
        queries, key_rows, FEATURE_DIMS, preferred_element_type=jnp.float32
    ) * jnp.exp(exponent)
    in_block = jnp.dot(scores.astype(jnp.bfloat16), values, preferred_element_type=jnp.float32)
    carried = jnp.where(segment == prev_seg, jnp.exp(cum_log), 0.0)
    last_seg = segment[row_count - 1]
    weights = jnp.where(
        segment == last_seg, jnp.exp(cum_log[row_count - 1] - cum_log + in_gate), 0.0
    )
    weighted = (key_rows.astype(jnp.float32) * weights[:, None]).astype(jnp.bfloat16)
    increment = lax.dot_general(weighted, values, ROW_DIMS, preferred_element_type=jnp.float32)
    block_decay = jnp.where(last_seg == prev_seg, jnp.exp(cum_log[row_count - 1]), 0.0)
    return (in_block, carried, increment, block_decay)


def end_state(
    state_in, key_rows, values, cum_log, in_gate, segment, seg_before, local_end, prompt, holder
):
    end_cum = cum_log[local_end]
    entering = jnp.where(holder & (seg_before == prompt), jnp.exp(end_cum), 0.0)
    row_order = jnp.arange(segment.shape[0])
    chosen = holder & (segment == prompt) & (row_order <= local_end)
    weights = jnp.where(chosen, jnp.exp(end_cum - cum_log + in_gate), 0.0)
    weighted = (key_rows.astype(jnp.float32) * weights[:, None]).astype(jnp.bfloat16)
    return entering * state_in + lax.dot_general(
        weighted, values, ROW_DIMS, preferred_element_type=jnp.float32
    )


def combine_states(earlier, later):
    return (earlier[0] * later[0], later[0] * earlier[1] + later[1])


def body(
    tokens,
    ln_gain,
    w_branch,
    w_outgate,
    w_gates,
    forget_bias,
    conv_weight,
    conv_bias,
    w_query,
    w_key,
    w_value,
    skip_gain,
    norm_gain,
    w_down,
    lengths,
    request_prompt,
):
    tok_rows = tokens.shape[0]
    seq_count = lax.axis_size("seq")
    seq_index = lax.axis_index("seq")
    head_idx = lax.axis_index("wr")
    row_offset = seq_index * tok_rows
    total_rows = tok_rows * seq_count
    row_ids = jnp.arange(tok_rows, dtype=jnp.int32)
    positions = row_offset + row_ids
    segment = segment_of(positions, lengths)
    seg_before = jnp.where(row_offset > 0, segment_of(row_offset - 1, lengths), -1)
    rim_positions = row_offset - (CONV - 1) + jnp.arange(CONV - 1, dtype=jnp.int32)
    rim_segment = jnp.where(rim_positions >= 0, segment_of(rim_positions, lengths), -1)
    ext_segment = jnp.concatenate([rim_segment, segment])
    prompt_starts = [jnp.zeros((), jnp.int32), lengths[0], lengths[0] + lengths[1]]
    prompt_ends = [
        lengths[0] - 1,
        lengths[0] + lengths[1] - 1,
        jnp.zeros((), jnp.int32) + (total_rows - 1),
    ]
    head_mask = (jnp.arange(HEADS, dtype=jnp.int32) == head_idx).astype(jnp.float32)
    current = tokens
    sent_states = []
    sent_edges = []
    for layer_idx in range(LAYERS):
        gathered = lax.all_gather(current, ("wr", "wc"), axis=1, tiled=True)
        normed = norm_rows(gathered, ln_gain[layer_idx])
        branch = jnp.dot(normed, w_branch[layer_idx], preferred_element_type=jnp.float32).astype(
            jnp.bfloat16
        )
        outgate = jnp.dot(normed, w_outgate[layer_idx], preferred_element_type=jnp.float32)
        gate_pre = jnp.dot(normed, w_gates[layer_idx], preferred_element_type=jnp.float32)
        input_pre = jnp.sum(gate_pre[:, :HEADS] * head_mask, axis=1)
        forget_pre = jnp.sum((gate_pre[:, HEADS:] + forget_bias[layer_idx]) * head_mask, axis=1)
        in_gate = GATE_CAP * jnp.tanh(input_pre / GATE_CAP)
        log_forget = jax.nn.log_sigmoid(forget_pre)
        edge_in = shifted(branch[tok_rows - (CONV - 1) :], "seq", 1)
        extended = jnp.concatenate([edge_in, branch], axis=0)
        conv_act = conv_rows(
            extended, ext_segment, segment, conv_weight[layer_idx], conv_bias[layer_idx]
        )
        head_branch, head_act = (
            lax.all_gather(branch, "wc", axis=1, tiled=True),
            lax.all_gather(conv_act, "wc", axis=1, tiled=True),
        )
        head_width = head_act.shape[1]
        queries = block_mix(head_act, w_query[layer_idx, 0]).astype(jnp.bfloat16)
        key_rows = (block_mix(head_act, w_key[layer_idx, 0]) * head_width ** (-0.5)).astype(
            jnp.bfloat16
        )
        values = block_mix(head_branch, w_value[layer_idx, 0]).astype(jnp.bfloat16)
        prefix = jnp.zeros((head_width, values.shape[1]), jnp.float32)
        reach_all = jnp.ones((), jnp.float32)
        in_block, carried, increment, block_decay = block_terms(
            queries, key_rows, values, log_forget, in_gate, segment, seg_before
        )
        saved_parts = (in_block, carried, reach_all, prefix)
        prefix = block_decay * prefix + increment
        reach_all = block_decay * reach_all
        entering = entering_2(
            (reach_all, prefix),
            "seq",
            combine_states,
            (jnp.ones((), jnp.float32), jnp.zeros_like(prefix)),
        )[1]
        in_block, carried, reach_here, prefix_here = saved_parts
        state_here = (reach_here * entering + prefix_here).astype(jnp.bfloat16)
        hidden_parts = in_block + carried[:, None] * jnp.dot(
            queries, state_here, preferred_element_type=jnp.float32
        )
        sums_one, sums_two = lax.psum(
            (jnp.sum(hidden_parts, axis=1), jnp.sum(hidden_parts * hidden_parts, axis=1)), "wc"
        )
        row_mean = sums_one / head_width
        row_var = sums_two / head_width - row_mean * row_mean
        normal_rows = (hidden_parts - row_mean[:, None]) * lax.rsqrt(row_var + EPSILON)[:, None]
        gated = (
            (
                normal_rows * norm_gain[layer_idx]
                + skip_gain[layer_idx] * conv_act.astype(jnp.float32)
            )
            * jax.nn.silu(outgate)
        ).astype(jnp.bfloat16)
        term_rows = jnp.dot(gated, w_down[layer_idx], preferred_element_type=jnp.float32)
        summed = lax.psum_scatter(
            term_rows.astype(jnp.bfloat16), ("wr", "wc"), scatter_dimension=1, tiled=True
        ).astype(jnp.float32)
        current = (current.astype(jnp.float32) + summed).astype(jnp.bfloat16)
        cum_log = jnp.cumsum(log_forget)
        for prompt in range(PROMPTS):
            end_pos = prompt_ends[prompt]
            holder = (end_pos >= row_offset) & (end_pos < row_offset + tok_rows)
            local_end = jnp.clip(end_pos - row_offset, 0, tok_rows - 1)
            state_end = end_state(
                entering,
                key_rows,
                values,
                cum_log,
                in_gate,
                segment,
                seg_before,
                local_end,
                prompt,
                holder,
            )
            window = lax.dynamic_slice_in_dim(extended, local_end + 1, CONV - 1, 0)
            edge_pos = end_pos - (CONV - 2) + jnp.arange(CONV - 1, dtype=jnp.int32)
            edge_rows = jnp.where(
                ((edge_pos >= prompt_starts[prompt]) & holder)[:, None],
                window,
                jnp.zeros_like(window),
            )
            got_state, got_edge = (
                broadcast(state_end.astype(jnp.bfloat16), "seq", end_pos // tok_rows),
                broadcast(edge_rows, "seq", end_pos // tok_rows),
            )
            sent_states.append(got_state)
            sent_edges.append(got_edge)
    state_stack = jnp.stack(sent_states)
    edge_stack = jnp.stack(sent_edges)
    state_stack = state_stack.reshape(LAYERS, PROMPTS, state_stack.shape[1], state_stack.shape[2])
    edge_stack = edge_stack.reshape(LAYERS, PROMPTS, edge_stack.shape[1], edge_stack.shape[2])
    chooser = (request_prompt[:, None] == jnp.arange(PROMPTS, dtype=jnp.int32)[None, :]).astype(
        jnp.bfloat16
    )
    request_state = jnp.einsum(
        "rp,lphd->lrhd", chooser, state_stack, preferred_element_type=jnp.float32
    ).astype(jnp.bfloat16)[:, :, None]
    request_conv = jnp.einsum(
        "rp,lpkc->lrkc", chooser, edge_stack, preferred_element_type=jnp.float32
    ).astype(jnp.bfloat16)
    return (current, request_state, request_conv)


def solution(mesh):
    return jax.shard_map(
        body,
        mesh=mesh,
        in_specs=(
            P("seq", ("wr", "wc")),
            P(),
            P(None, None, ("wr", "wc")),
            P(None, None, ("wr", "wc")),
            P(),
            P(),
            P(None, None, ("wr", "wc")),
            P(None, ("wr", "wc")),
            P(None, "wr", None, None, None),
            P(None, "wr", None, None, None),
            P(None, "wr", None, "wc", None),
            P(None, ("wr", "wc")),
            P(None, ("wr", "wc")),
            P(None, ("wr", "wc"), None),
            P(),
            P("seq"),
        ),
        out_specs=(
            P("seq", ("wr", "wc")),
            P(None, "seq", "wr", None, "wc"),
            P(None, "seq", None, ("wr", "wc")),
        ),
        check_vma=False,
    )
```

profile of v0, /device:TPU:8, one launch (start us, length us, event | category | flops | bytes accessed | tf_op | source)
XLA Modules:
  0.0 1086.0 jit_solution(4009449505985787538)
XLA Ops:
  14.7 1.5 fusion.229
  17.0 47.1 %all-gather.11.cloned.1.call-done = bf16[512,2048]{1,0:T(8,128)(2,1)} async-done(((bf16[512,128]{1,0:T(8,128)(2,1)}), bf16[512,2048]{1,0:T(8,128)(2,1)}) %all-gather.11.cloned.1.call-update) | async-done | bytes 2097168 | tf_op jit(solution)/shard_map/all_gather | solution.py:163
  64.1 2.4 convert_reduce_fusion.1
  68.1 1.4 convolution_convert_fusion.5
  71.5 2.5 collective-permute-start
  82.0 1.8 tanh_multiply_fusion.1
  83.8 8.9 all-gather.15.cloned.1.call-done
  92.7 1.9 reshape.476
  94.5 2.1 multiply_reduce_fusion.1
  97.7 19.7 %all-gather.13.cloned.1.call-done = bf16[512,1024]{1,0:T(8,128)(2,1)} async-done(((bf16[512,256]{1,0:T(8,128)(2,1)}), bf16[512,1024]{1,0:T(8,128)(2,1)}) %all-gather.13.cloned.1.call-update) | async-done | bytes 1048592 | tf_op jit(solution)/shard_map/all_gather | solution.py:181
  117.4 2.6 reshape.474
  120.0 2.8 copy.89
  122.8 4.2 fusion.99
  127.0 2.9 copy.92
  129.9 3.2 fusion.16
  133.2 2.4 copy.95
  135.5 2.5 fusion.30
  141.2 2.0 dynamic-update-slice
  144.2 38.1 %all-reduce = bf16[16]{0:T(256)(128)(2,1)S(1)} all-reduce(bf16[16]{0:T(256)(128)(2,1)} %dynamic-update-slice), channel_id=1, replica_groups=mesh['seq'=16,'wr'=4,'wc'=4] {'seq'}, use_global_device_ids=true, to_apply=%add | all-reduce | flops 16 | bytes 64
  182.3 2.9 fusion.26
  187.8 3.2 fusion.53
  191.0 130.3 %all-gather.23.cloned.1.call-done = bf16[16384,256]{1,0:T(8,128)(2,1)} async-done(((bf16[1024,256]{1,0:T(8,128)(2,1)}), bf16[16384,256]{1,0:T(8,128)(2,1)}) %all-gather.23.cloned.1.call-update) | async-done | bytes 8388624 | tf_op jit(solution)/shard_map/all_gather | solution.py:27
  322.1 2.7 fusion.217
  324.8 9.4 all-reduce.3
  334.9 5.5 convolution_convert_fusion.1
  340.4 3.9 copy.136
  344.4 114.9 %reduce-scatter.7.cloned.1.call-done = bf16[128,512]{1,0:T(8,128)(2,1)} async-done(((bf16[2048,512]{1,0:T(8,128)(2,1)}), bf16[128,512]{1,0:T(8,128)(2,1)}) %reduce-scatter.7.cloned.1.call-update) | async-done | bytes 131088
  461.1 51.2 %all-gather.17.cloned.1.call-done = bf16[512,2048]{1,0:T(8,128)(2,1)} async-done(((bf16[512,128]{1,0:T(8,128)(2,1)}), bf16[512,2048]{1,0:T(8,128)(2,1)}) %all-gather.17.cloned.1.call-update) | async-done | bytes 2097168 | tf_op jit(solution)/shard_map/all_gather | solution.py:163
  512.3 2.4 convert_reduce_fusion
  516.4 1.4 convolution_convert_fusion.4
  518.6 2.5 collective-permute-start.1
  523.4 1.8 multiply_convert_fusion.3
  529.3 3.2 exponential_select_fusion.1
  532.5 8.4 all-gather.21.cloned.1.call-done
  540.9 1.9 reshape.480
  542.8 1.4 multiply_reduce_fusion
  545.0 20.6 %all-gather.19.cloned.1.call-done = bf16[512,1024]{1,0:T(8,128)(2,1)} async-done(((bf16[512,256]{1,0:T(8,128)(2,1)}), bf16[512,1024]{1,0:T(8,128)(2,1)}) %all-gather.19.cloned.1.call-update) | async-done | bytes 1048592 | tf_op jit(solution)/shard_map/all_gather | solution.py:181
  565.6 1.9 reshape.478
  567.5 1.4 copy.99
  568.9 4.2 fusion.96
  573.1 2.9 copy.102
  576.0 2.8 fusion.23
  578.9 1.8 fusion.22
  580.7 2.3 copy.105
  583.0 2.5 fusion.31
  590.7 71.5 %all-reduce.4 = (bf16[16]{0:T(256)(128)(2,1)S(1)}, bf16[1,3,256]{2,1,0:T(4,128)(2,1)S(1)}, bf16[1,3,256]{2,1,0:T(4,128)(2,1)S(1)}, bf16[1,3,256]{2,1,0:T(4,128)(...) all-reduce(bf16[16]{0:T(256)(128)(2,1)S(1)} %dynamic-update-slice.1, ...), channel_id=1, replica_groups=mesh['seq'=16,'wr'=4,'wc'=4] {'seq'}, use_global_device_ids=true, to_apply=%add.1 | all-reduce | flops 4624 | bytes 18496
  662.2 2.9 fusion.27
  667.5 3.3 fusion.52
  670.8 99.3 %all-gather.25.cloned.1.call-done = bf16[16384,256]{1,0:T(8,128)(2,1)} async-done(((bf16[1024,256]{1,0:T(8,128)(2,1)}), bf16[16384,256]{1,0:T(8,128)(2,1)}) %all-gather.25.cloned.1.call-update) | async-done | bytes 8388624 | tf_op jit(solution)/shard_map/all_gather | solution.py:27
  770.5 2.7 fusion.216
  773.1 8.8 all-reduce.2
  782.0 6.1 convolution_convert_fusion
  788.1 3.9 copy.138
  796.2 1.9 exponential_select_fusion.3
  798.1 3.4 fusion.19
  801.5 2.3 copy.110
  803.8 2.3 copy.109
  806.0 2.3 copy.108
  808.3 2.6 fusion.47
  813.5 2.4 copy.113
  823.8 82.0 %reduce-scatter.9.cloned.1.call-done = bf16[128,512]{1,0:T(8,128)(2,1)} async-done(((bf16[2048,512]{1,0:T(8,128)(2,1)}), bf16[128,512]{1,0:T(8,128)(2,1)}) %reduce-scatter.9.cloned.1.call-update) | async-done | bytes 131088
  907.5 164.4 %all-reduce.8.cloned.1.call-done = (bf16[1,1024,256]{2,1,0:T(8,128)(2,1)}, bf16[1,1024,256]{2,1,0:T(8,128)(2,1)}, bf16[1,1024,256]{2,1,0:T(8,128)(2,1)}, bf16[1,...) async-done(((bf16[1,1024,256]{2,1,0:T(8,128)(2,1)}, bf16[1,1024,256]{2,1,0:T(8,128)(2,1)}, bf16[1,1024,256]{2,1,0:T(8,128)(2,1)}, ...) | async-done | bytes 3145744 | tf_op jit(solution)/shard_map/psum | solution.py:46
  1074.5 3.1 fusion.13
  1077.6 1.6 copy.116
  (214 shorter events, 57.2 us)
Async XLA Ops:
  7.2 56.9 %all-gather.11.cloned.1.call-start = ((), (), s32[]{:S(2)}) async-start(), calls=%async_computation.2 | async-start | bytes 2228224 | tf_op jit(solution)/shard_map/all_gather | solution.py:163
  7.9 84.8 %all-gather.15.cloned.1.call-start = ((), (), s32[]{:S(2)}) async-start(), calls=%async_computation.4 | async-start | bytes 1310720 | tf_op jit(solution)/shard_map/all_gather | solution.py:180
  11.3 59.7 %copy-start.39 = (f32[4]{0:T(128)}, f32[4]{0:T(128)S(1)}, u32[]{:S(2)}) copy-start(f32[4]{0:T(128)S(1)} %compare_convert_fusion) | copy-start | bytes 52
  64.1 2.5 copy-start.1
  66.5 1.6 copy-start.46
  68.1 2.2 copy-start.22
  69.6 6.1 copy-start.15
  69.6 47.8 %all-gather.13.cloned.1.call-start = ((), (), s32[]{:S(2)}) async-start(), calls=%async_computation.3 | async-start | bytes 1310720 | tf_op jit(solution)/shard_map/all_gather | solution.py:181
  71.0 6.7 copy-start.29
  71.0 7.3 copy-start.23
  71.1 10.8 copy-start.24
  71.5 4.1 collective-permute-start
  75.5 8.3 copy-start.30
  75.7 8.1 copy-start.27
  76.9 244.4 %all-gather.23.cloned.1.call-start = ((), (), s32[]{:S(2)}) async-start(), calls=%async_computation.8 | async-start | bytes 8912896 | tf_op jit(solution)/shard_map/all_gather | solution.py:27
  133.1 4.9 copy-start.49
  133.1 5.5 copy-start.41
  133.2 6.1 copy-start.42
  138.0 321.3 %reduce-scatter.7.cloned.1.call-start = ((), (), s32[]{:S(2)}) async-start(), calls=%async_computation.10 | async-start | bytes 2228224
  182.3 5.1 copy-start.31
  182.3 5.1 copy-start.38
  185.3 1.0 copy-start.12
  186.2 1.5 copy-start.4
  321.4 0.7 copy-start.33
  344.3 116.0 %copy-start.17 = (bf16[512,128]{1,0:T(8,128)(2,1)S(1)}, bf16[512,128]{1,0:T(8,128)(2,1)}, u32[]{:S(2)}) copy-start(bf16[512,128]{1,0:T(8,128)(2,1)} %param.20) | copy-start | bytes 393220
  344.3 168.0 %all-gather.17.cloned.1.call-start = ((), (), s32[]{:S(2)}) async-start(), calls=%async_computation.5 | async-start | bytes 2228224 | tf_op jit(solution)/shard_map/all_gather | solution.py:163
  461.0 79.9 %all-gather.21.cloned.1.call-start = ((), (), s32[]{:S(2)}) async-start(), calls=%async_computation.7 | async-start | bytes 1310720 | tf_op jit(solution)/shard_map/all_gather | solution.py:180
  512.3 2.5 copy-start.2
  514.8 1.6 copy-start.47
  516.4 10.1 copy-start
  516.4 7.0 copy-start.34
  516.4 7.0 copy-start.35
  516.4 7.0 copy-start.36
  516.4 7.0 copy-start.37
  517.8 7.6 copy-start.26
  517.8 47.8 %all-gather.19.cloned.1.call-start = ((), (), s32[]{:S(2)}) async-start(), calls=%async_computation.6 | async-start | bytes 1310720 | tf_op jit(solution)/shard_map/all_gather | solution.py:181
  518.6 3.8 collective-permute-start.1
  525.2 2.0 copy-start.40
  525.2 2.0 copy-start.43
  525.2 244.9 %all-gather.25.cloned.1.call-start = ((), (), s32[]{:S(2)}) async-start(), calls=%async_computation.9 | async-start | bytes 8912896 | tf_op jit(solution)/shard_map/all_gather | solution.py:27
  578.9 1.8 copy-start.5
  583.0 5.1 copy-start.28
  585.6 320.2 %reduce-scatter.9.cloned.1.call-start = ((), (), s32[]{:S(2)}) async-start(), calls=%async_computation.11 | async-start | bytes 2228224
  662.2 5.1 copy-start.32
  665.1 1.0 copy-start.10
  666.0 1.5 copy-start.6
  770.4 11.5 %copy-start.44 = (f32[1,256]{1,0:T(1,128)S(1)}, f32[1,256]{1,0:T(1,128)}, u32[]{:S(2)}) copy-start(f32[1,256]{1,0:T(1,128)} %get-tuple-element.222) | copy-start | bytes 3076
  770.4 11.5 %copy-start.45 = (f32[1,256]{1,0:T(1,128)S(1)}, f32[1,256]{1,0:T(1,128)}, u32[]{:S(2)}) copy-start(f32[1,256]{1,0:T(1,128)} %get-tuple-element.220) | copy-start | bytes 3076
  792.0 4.2 copy-start.25
  792.0 280.0 %all-reduce.8.cloned.1.call-start = ((), (), s32[]{:S(2)}) async-start(), calls=%async_computation.12 | async-start | bytes 6291456 | tf_op jit(solution)/shard_map/psum | solution.py:46
  808.3 2.6 copy-start.8
  810.9 1.3 copy-start.7
  813.5 2.4 copy-start.3
  815.9 2.7 copy-start.14
  817.2 1.3 copy-start.13
  818.5 1.3 copy-start.11
  819.8 1.3 copy-start.9
  822.3 0.7 copy-start.48
  822.3 84.5 %copy-start.16 = (bf16[512,128]{1,0:T(8,128)(2,1)S(1)}, bf16[512,128]{1,0:T(8,128)(2,1)}, u32[]{:S(2)}) copy-start(bf16[512,128]{1,0:T(8,128)(2,1)} %add_convert_fusion.1) | copy-start | bytes 393220
  1072.0 2.4 copy-start.21
  1072.0 2.4 copy-start.20
  1072.0 2.5 copy-start.19
  1073.2 1.3 copy-start.18
Sparse Core Ops, SparseCore 0:
  10.6 53.4 all-gather.10
  69.7 22.9 all-gather.14
  94.5 22.8 all-gather.12
  138.1 183.1 all-gather.22
  344.4 114.8 reduce-scatter.6
  462.3 49.9 all-gather.16
  518.0 22.8 all-gather.20
  542.7 22.8 all-gather.18
  585.7 184.3 all-gather.24
  792.1 113.6 reduce-scatter.8
  908.9 162.9 all-reduce.7
where the time goes:
time: 1100 us; the launch traced here: 1090 us
  waiting for transfers between devices  749 us (68%)
  blocking collectives  128 us (12%)
  local copies, waits for them, and re-layouts  79.5 us (7%)
  matrix products  59.7 us (5%)
  other arithmetic  39.7 us (4%)
  between operations  24.4 us (2%)
    all_gather x2, waiting for transfers between devices, entering_2(): lax.all_gather(a.astype(kind), axis)  230 us
    unnamed x13, waiting for transfers between devices  198 us
    psum x1, waiting for transfers between devices, broadcast(): return lax.psum(jnp.where(mine, shard, jnp.zeros_like(shard)), axis)  164 us
    unnamed x2, blocking collectives  110 us
    all_gather x2, waiting for transfers between devices, body(): gathered = lax.all_gather(current, ('wr', 'wc'), axis=1, tiled=True)  98.3 us
    all_gather x2, waiting for transfers between devices, body(): lax.all_gather(conv_act, 'wc', axis=1, tiled=True)  40.3 us
    unnamed x126, local copies, waits for them, and re-layouts  27.7 us
  transfers between devices with their start and end apart: 13, of which 12 were waited for; matrix products, arithmetic and copies ran while one was open for 8% of the time, Pallas kernels for 0%

commit v1 on v0

--- a/solution.py
+++ b/solution.py
@@ -21,29 +21,32 @@
     return lax.ppermute(value, axis, [(source, source + steps) for source in range(first, last)])
 
 
-def entering_2(shard, axis, join, neutral):
-    place = lax.axis_index(axis)
-    gathered = jax.tree.map(
-        lambda a, kind: lax.all_gather(a.astype(kind), axis), shard, (jnp.bfloat16, jnp.bfloat16)
-    )
-    state = jax.tree.map(lambda a, e: jnp.zeros_like(a) + jnp.asarray(e, a.dtype), shard, neutral)
-
-    def one(step, state):
-        return join(
-            state,
-            jax.tree.map(
-                lambda a, own: lax.dynamic_index_in_dim(a, step, 0, False).astype(own.dtype),
-                gathered,
-                shard,
-            ),
-        )
-
-    return lax.fori_loop(0, place, one, state)
-
-
-def broadcast(shard, axis, root):
-    mine = lax.axis_index(axis) == root
-    return lax.psum(jnp.where(mine, shard, jnp.zeros_like(shard)), axis)
+def span_weights(gathered, lengths, rows, count):
+    spans = jnp.arange(count, dtype=jnp.int32)
+    seg_end = segment_of(spans * rows + (rows - 1), lengths)
+    totals = gathered[:, 0]
+    later = jnp.arange(count + 1, dtype=jnp.int32)
+    between = (spans[None, None, :] > spans[None, :, None]) & (
+        spans[None, None, :] < later[:, None, None]
+    )
+    logs = jnp.sum(jnp.where(between, totals[None, None, :], 0.0), axis=2)
+    seg_in = segment_of(later * rows - 1, lengths)
+    keep = (spans[None, :] < later[:, None]) & (seg_end[None, :] == seg_in[:, None])
+    state_rows = jnp.where(keep, jnp.exp(logs), 0.0)
+    end_rows = []
+    for prompt, end_pos in enumerate((lengths[0] - 1, lengths[0] + lengths[1] - 1)):
+        holder = end_pos // rows
+        pick = (spans == holder).astype(jnp.float32)
+        end_cum = jnp.sum(pick * gathered[:, 1 + prompt])
+        row = jnp.sum(pick[:, None] * logs[:count], axis=0) + end_cum
+        kept = (spans < holder) & (seg_end == prompt)
+        kept = kept & (segment_of(holder * rows - 1, lengths) == prompt)
+        end_rows.append(jnp.where(kept, jnp.exp(row), 0.0))
+    return state_rows[:count], jnp.stack(end_rows + [state_rows[count]])
+
+
+def mix_spans(weights, spans):
+    return jnp.sum(weights[:, :, None, None] * spans[None], axis=1)
 
 
 def norm_rows(source, gain_row):
@@ -96,26 +99,15 @@
     )
     weighted = (key_rows.astype(jnp.float32) * weights[:, None]).astype(jnp.bfloat16)
     increment = lax.dot_general(weighted, values, ROW_DIMS, preferred_element_type=jnp.float32)
-    block_decay = jnp.where(last_seg == prev_seg, jnp.exp(cum_log[row_count - 1]), 0.0)
-    return (in_block, carried, increment, block_decay)
-
-
-def end_state(
-    state_in, key_rows, values, cum_log, in_gate, segment, seg_before, local_end, prompt, holder
-):
-    end_cum = cum_log[local_end]
-    entering = jnp.where(holder & (seg_before == prompt), jnp.exp(end_cum), 0.0)
+    return (in_block, carried, increment)
+
+
+def end_part(key_rows, values, cum_log, in_gate, segment, local_end, prompt, holder):
     row_order = jnp.arange(segment.shape[0])
     chosen = holder & (segment == prompt) & (row_order <= local_end)
-    weights = jnp.where(chosen, jnp.exp(end_cum - cum_log + in_gate), 0.0)
+    weights = jnp.where(chosen, jnp.exp(cum_log[local_end] - cum_log + in_gate), 0.0)
     weighted = (key_rows.astype(jnp.float32) * weights[:, None]).astype(jnp.bfloat16)
-    return entering * state_in + lax.dot_general(
-        weighted, values, ROW_DIMS, preferred_element_type=jnp.float32
-    )
-
-
-def combine_states(earlier, later):
-    return (earlier[0] * later[0], later[0] * earlier[1] + later[1])
+    return lax.dot_general(weighted, values, ROW_DIMS, preferred_element_type=jnp.float32)
 
 
 def body(
@@ -186,22 +178,47 @@
             jnp.bfloat16
         )
         values = block_mix(head_branch, w_value[layer_idx, 0]).astype(jnp.bfloat16)
-        prefix = jnp.zeros((head_width, values.shape[1]), jnp.float32)
-        reach_all = jnp.ones((), jnp.float32)
-        in_block, carried, increment, block_decay = block_terms(
+        cum_log = jnp.cumsum(log_forget)
+        holders = [
+            (end_pos >= row_offset) & (end_pos < row_offset + tok_rows) for end_pos in prompt_ends
+        ]
+        local_ends = [jnp.clip(end_pos - row_offset, 0, tok_rows - 1) for end_pos in prompt_ends]
+        span_logs = lax.all_gather(
+            jnp.stack([cum_log[tok_rows - 1], cum_log[local_ends[0]], cum_log[local_ends[1]]]),
+            "seq",
+        )
+        state_rows, end_rows = span_weights(span_logs, lengths, tok_rows, seq_count)
+        in_block, carried, increment = block_terms(
             queries, key_rows, values, log_forget, in_gate, segment, seg_before
         )
-        saved_parts = (in_block, carried, reach_all, prefix)
-        prefix = block_decay * prefix + increment
-        reach_all = block_decay * reach_all
-        entering = entering_2(
-            (reach_all, prefix),
-            "seq",
-            combine_states,
-            (jnp.ones((), jnp.float32), jnp.zeros_like(prefix)),
-        )[1]
-        in_block, carried, reach_here, prefix_here = saved_parts
-        state_here = (reach_here * entering + prefix_here).astype(jnp.bfloat16)
+        parts = [increment] + [
+            end_part(
+                key_rows,
+                values,
+                cum_log,
+                in_gate,
+                segment,
+                local_ends[prompt],
+                prompt,
+                holders[prompt],
+            )
+            for prompt in range(PROMPTS - 1)
+        ]
+        slab = head_width // seq_count
+        sent = jnp.stack(
+            [part.astype(jnp.bfloat16).reshape(seq_count, slab, -1) for part in parts], axis=1
+        )
+        got = lax.all_to_all(sent, "seq", 0, 0, tiled=True).astype(jnp.float32)
+        spans = got[:, 0]
+        states = mix_spans(state_rows, spans).astype(jnp.bfloat16)
+        state_here = lax.all_to_all(states, "seq", 0, 0, tiled=True).reshape(head_width, -1)
+        own_ends = jnp.sum(got[:, 1:], axis=0)
+        ends = mix_spans(end_rows, spans) + jnp.concatenate(
+            [own_ends, jnp.zeros_like(own_ends[:1])], axis=0
+        )
+        sent_states.append(
+            lax.all_gather(ends.astype(jnp.bfloat16), "seq", axis=1, tiled=True)
+        )
         hidden_parts = in_block + carried[:, None] * jnp.dot(
             queries, state_here, preferred_element_type=jnp.float32
         )
@@ -219,43 +236,25 @@
             * jax.nn.silu(outgate)
         ).astype(jnp.bfloat16)
         term_rows = jnp.dot(gated, w_down[layer_idx], preferred_element_type=jnp.float32)
-        summed = lax.psum_scatter(
-            term_rows.astype(jnp.bfloat16), ("wr", "wc"), scatter_dimension=1, tiled=True
-        ).astype(jnp.float32)
+        terms = lax.all_to_all(
+            term_rows.astype(jnp.bfloat16), ("wr", "wc"), 1, 0, tiled=True
+        ).reshape(-1, tok_rows, current.shape[1])
+        summed = jnp.sum(terms.astype(jnp.float32), axis=0)
         current = (current.astype(jnp.float32) + summed).astype(jnp.bfloat16)
-        cum_log = jnp.cumsum(log_forget)
         for prompt in range(PROMPTS):
-            end_pos = prompt_ends[prompt]
-            holder = (end_pos >= row_offset) & (end_pos < row_offset + tok_rows)
-            local_end = jnp.clip(end_pos - row_offset, 0, tok_rows - 1)
-            state_end = end_state(
-                entering,
-                key_rows,
-                values,
-                cum_log,
-                in_gate,
-                segment,
-                seg_before,
-                local_end,
-                prompt,
-                holder,
-            )
-            window = lax.dynamic_slice_in_dim(extended, local_end + 1, CONV - 1, 0)
-            edge_pos = end_pos - (CONV - 2) + jnp.arange(CONV - 1, dtype=jnp.int32)
-            edge_rows = jnp.where(
-                ((edge_pos >= prompt_starts[prompt]) & holder)[:, None],
-                window,
-                jnp.zeros_like(window),
-            )
-            got_state, got_edge = (
-                broadcast(state_end.astype(jnp.bfloat16), "seq", end_pos // tok_rows),
-                broadcast(edge_rows, "seq", end_pos // tok_rows),
-            )
-            sent_states.append(got_state)
-            sent_edges.append(got_edge)
+            window = lax.dynamic_slice_in_dim(extended, local_ends[prompt] + 1, CONV - 1, 0)
+            edge_pos = (
+                prompt_ends[prompt] - (CONV - 2) + jnp.arange(CONV - 1, dtype=jnp.int32)
+            )
+            sent_edges.append(
+                jnp.where(
+                    ((edge_pos >= prompt_starts[prompt]) & holders[prompt])[:, None],
+                    window,
+                    jnp.zeros_like(window),
+                )
+            )
     state_stack = jnp.stack(sent_states)
-    edge_stack = jnp.stack(sent_edges)
-    state_stack = state_stack.reshape(LAYERS, PROMPTS, state_stack.shape[1], state_stack.shape[2])
+    edge_stack = lax.psum(jnp.stack(sent_edges), "seq")
     edge_stack = edge_stack.reshape(LAYERS, PROMPTS, edge_stack.shape[1], edge_stack.shape[2])
     chooser = (request_prompt[:, None] == jnp.arange(PROMPTS, dtype=jnp.int32)[None, :]).astype(
         jnp.bfloat16

time: 1100 us -> 670 us (0.61)
  waiting for transfers between devices: 749 us -> 158 us
  blocking collectives: 128 us -> 245 us
  starting transfers between devices: 5.55 us -> 41.3 us
  other arithmetic: 39.7 us -> 69.9 us
    all_gather x2, waiting for transfers between devices: 230 us -> 0.01 us  [body(): lax.all_gather(ends.astype(jnp.bfloat16), 'seq', axis=1, tiled=True)]
    unnamed x13 -> x8, waiting for transfers between devices: 198 us -> 0.8 us
    psum x1 -> x0, waiting for transfers between devices: 164 us -> none  [broadcast(): return lax.psum(jnp.where(mine, shard, jnp.zeros_like(shard)), axis)]
    psum x0 -> x1, blocking collectives: none -> 82.8 us  [body(): edge_stack = lax.psum(jnp.stack(sent_edges), 'seq')]
    all_to_all x0 -> x5, starting transfers between devices: none -> 35.6 us  [the longest x2 14.6 us: body(): got = lax.all_to_all(sent, 'seq', 0, 0, tiled=True).astype(jnp.float32)]
    all_to_all x0 -> x1, blocking collectives: none -> 32.7 us  [body(): lax.all_to_all(term_rows.astype(jnp.bfloat16), ('wr', 'wc'), 1, 0, tiled=...]
    reduce_sum x0 -> x13, other arithmetic: none -> 13.4 us  [the longest x4 9.45 us: mix_spans(): return jnp.sum(weights[:, :, None, None] * spans[None], axis=1)]
    unnamed x126 -> x154, local copies, waits for them, and re-layouts: 27.7 us -> 15 us
  transfers between devices with their start and end apart: 13 -> 15, of which waited for: 12 -> 9; matrix products, arithmetic and copies ran while one was open for 8% -> 16% of each run, Pallas kernels for 0% -> 0%
where the time goes in v1:
time: 670 us; the launch traced here: 663 us
  blocking collectives  245 us (37%)
  waiting for transfers between devices  158 us (24%)
  local copies, waits for them, and re-layouts  72 us (11%)
  other arithmetic  69.9 us (10%)
  matrix products  56.6 us (8%)
  starting transfers between devices  41.3 us (6%)
  between operations  20.7 us (3%)
    unnamed x2, blocking collectives  115 us
    all_gather x2, waiting for transfers between devices, body(): gathered = lax.all_gather(current, ('wr', 'wc'), axis=1, tiled=True)  96 us
    psum x1, blocking collectives, body(): edge_stack = lax.psum(jnp.stack(sent_edges), 'seq')  82.8 us
    all_gather x2, waiting for transfers between devices, body(): lax.all_gather(conv_act, 'wc', axis=1, tiled=True)  38.8 us
    all_to_all x1, blocking collectives, body(): lax.all_to_all(term_rows.astype(jnp.bfloat16), ('wr', 'wc'), 1, 0, tiled=...  32.7 us
    unnamed x154, local copies, waits for them, and re-layouts  15 us
    all_to_all x2, starting transfers between devices, body(): got = lax.all_to_all(sent, 'seq', 0, 0, tiled=True).astype(jnp.float32)  14.6 us
    psum x2, blocking collectives, body(): lax.psum((jnp.sum(hidden_parts, axis=1), jnp.sum(hidden_parts * hidden_pa...  14.5 us
  transfers between devices with their start and end apart: 15, of which 9 were waited for; matrix products, arithmetic and copies ran while one was open for 16% of the time, Pallas kernels for 0%

profile of v1, /device:TPU:8, one launch (start us, length us, event | category | flops | bytes accessed | tf_op | source)
XLA Modules:
  0.0 662.9 jit_solution(5510766327636577990)
XLA Ops:
  14.5 49.5 %all-gather.11.cloned.1.call-done = bf16[512,2048]{1,0:T(8,128)(2,1)} async-done(((bf16[512,128]{1,0:T(8,128)(2,1)}), bf16[512,2048]{1,0:T(8,128)(2,1)}) %all-gather.11.cloned.1.call-update) | async-done | bytes 2097168 | tf_op jit(solution)/shard_map/all_gather | solution.py:155
  64.1 2.4 convert_reduce_fusion.1
  72.9 2.8 collective-permute-start
  83.4 3.7 exponential_select_fusion.7
  87.1 5.6 all-gather.15.cloned.1.call-done
  92.7 1.9 reshape.611
  96.1 21.3 %all-gather.13.cloned.1.call-done = bf16[512,1024]{1,0:T(8,128)(2,1)} async-done(((bf16[512,256]{1,0:T(8,128)(2,1)}), bf16[512,1024]{1,0:T(8,128)(2,1)}) %all-gather.13.cloned.1.call-update) | async-done | bytes 1048592 | tf_op jit(solution)/shard_map/all_gather | solution.py:173
  117.4 1.9 reshape.609
  120.6 3.3 fusion.74
  123.9 1.8 copy.185
  125.7 1.9 fusion.11
  136.1 7.3 %all-to-all-start = ((bf16[16,3,64,256]{3,2,1,0:T(8,128)(2,1)}), bf16[16,3,64,256]{3,2,1,0:T(8,128)(2,1)}, u32[]{:S(2)}, u32[]{:S(2)}) async-start(bf16[16,3,64,256]{3,2,1,0:T(8,128)(2,1)} %pad_maximum_fusion.6), calls=%async_computation | async-start | bytes 3145728 | tf_op jit(solution)/shard_map/all_to_all | solution.py:211
  147.7 2.0 maximum_dynamic-update-slice_fusion
  149.8 56.5 %all-reduce.2 = f32[48]{0:T(128)S(1)} all-reduce(f32[48]{0:T(128)S(1)} %maximum_dynamic-update-slice_fusion), channel_id=2, replica_groups=mesh['seq'=16,'wr'=4,'wc'=4] {'seq'}, use_global_device_ids=true, to_apply=%add.2 | all-reduce | flops 48 | bytes 384
  207.5 1.8 convert_element_type.500
  210.4 3.2 multiply_reduce_fusion.1
  213.5 6.7 %all-to-all-start.1 = ((bf16[16,64,256]{2,1,0:T(8,128)(2,1)}), bf16[16,64,256]{2,1,0:T(8,128)(2,1)}, u32[]{:S(2)}, u32[]{:S(2)}) async-start(bf16[16,64,256]{2,1,0:T(8,128)(2,1)} %multiply_reduce_fusion.1), calls=%async_computation.1 | async-start | bytes 1048576 | tf_op jit(solution)/shard_map/all_to_all | solution.py:214
  221.5 3.2 fusion.21
  226.9 3.5 fusion.28
  230.5 3.3 all-to-all-done.1
  233.8 2.8 fusion.186
  236.6 7.1 %all-reduce.5 = (f32[512]{0:T(512)S(1)}, f32[512]{0:T(512)S(1)}) all-reduce(f32[512]{0:T(512)S(1)} %get-tuple-element.28, f32[512]{0:T(512)S(1)} %get-tuple-element.27), channel_id=1, replica_groups=mesh['seq'=16,'wr'=4,'wc'=4] {'wc'}, use_global_device_ids=true, to_apply=%region_11.12 | all-reduce | flops 1024 | bytes 8192 | tf_op jit(solution)/shard_map/psum | solution.py:225
  243.7 6.0 fusion.17
  249.8 2.1 copy.269
  251.9 32.7 %all_to_all.46 = bf16[512,16,128]{2,0,1:T(8,128)(2,1)S(1)} all-to-all(bf16[512,16,128]{2,0,1:T(8,128)(2,1)S(1)} %bitcast.288), channel_id=1, replica_groups=mesh['seq'=16,'wr'=4,'wc'=4] {'wr','wc'}, dimensions={1} | all-to-all | bytes 4194304 | tf_op jit(solution)/shard_map/all_to_all | solution.py:239
  286.5 46.4 %all-gather.17.cloned.1.call-done = bf16[512,2048]{1,0:T(8,128)(2,1)} async-done(((bf16[512,128]{1,0:T(8,128)(2,1)}), bf16[512,2048]{1,0:T(8,128)(2,1)}) %all-gather.17.cloned.1.call-update) | async-done | bytes 2097168 | tf_op jit(solution)/shard_map/all_gather | solution.py:155
  332.9 2.4 convert_reduce_fusion
  339.6 2.5 collective-permute-start.1
  347.4 2.2 fusion.131
  351.6 2.5 exponential_select_fusion.3
  354.1 7.9 %all-gather.21.cloned.1.call-done = bf16[512,1024]{1,0:T(8,128)(2,1)} async-done(((bf16[512,256]{1,0:T(8,128)(2,1)}), bf16[512,1024]{1,0:T(8,128)(2,1)}) %all-gather.21.cloned.1.call-update) | async-done | bytes 1048592 | tf_op jit(solution)/shard_map/all_gather | solution.py:172
  362.0 2.6 reshape.616
  364.6 3.4 multiply_reduce_fusion.4
  369.1 17.5 %all-gather.19.cloned.1.call-done = bf16[512,1024]{1,0:T(8,128)(2,1)} async-done(((bf16[512,256]{1,0:T(8,128)(2,1)}), bf16[512,1024]{1,0:T(8,128)(2,1)}) %all-gather.19.cloned.1.call-update) | async-done | bytes 1048592 | tf_op jit(solution)/shard_map/all_gather | solution.py:173
  386.5 2.6 reshape.614
  389.2 3.8 copy.199
  393.0 4.5 fusion.71
  397.6 2.9 copy.202
  400.4 3.2 fusion.14
  403.6 2.3 copy.206
  405.9 3.0 fusion.15
  408.9 2.3 copy.207
  411.2 2.5 convolution_convert_fusion.6
  413.7 2.5 convolution_convert_fusion.5
  416.2 2.3 copy.208
  421.7 7.3 %all-to-all-start.3 = ((bf16[16,3,64,256]{3,2,1,0:T(8,128)(2,1)}), bf16[16,3,64,256]{3,2,1,0:T(8,128)(2,1)}, u32[]{:S(2)}, u32[]{:S(2)}) async-start(bf16[16,3,64,256]{3,2,1,0:T(8,128)(2,1)} %pad_maximum_fusion.7), calls=%async_computation.3 | async-start | bytes 3145728 | tf_op jit(solution)/shard_map/all_to_all | solution.py:211
  431.8 2.0 maximum_dynamic-update-slice_fusion.1
  433.8 58.0 %all-reduce.3 = f32[48]{0:T(128)S(1)} all-reduce(f32[48]{0:T(128)S(1)} %maximum_dynamic-update-slice_fusion.1), channel_id=3, replica_groups=mesh['seq'=16,'wr'=4,'wc'=4] {'seq'}, use_global_device_ids=true, to_apply=%add.3 | all-reduce | flops 48 | bytes 384
  499.1 1.8 copy.249
  503.2 1.8 convert_element_type.533
  506.1 3.1 multiply_reduce_fusion
  509.3 6.7 %all-to-all-start.4 = ((bf16[16,64,256]{2,1,0:T(8,128)(2,1)}), bf16[16,64,256]{2,1,0:T(8,128)(2,1)}, u32[]{:S(2)}, u32[]{:S(2)}) async-start(bf16[16,64,256]{2,1,0:T(8,128)(2,1)} %multiply_reduce_fusion), calls=%async_computation.4 | async-start | bytes 1048576 | tf_op jit(solution)/shard_map/all_to_all | solution.py:214
  516.1 3.2 fusion.22
  521.5 3.6 fusion.27
  527.6 4.3 all-to-all-done.4
  531.9 2.2 fusion.185
  534.1 7.3 %all-reduce.4 = (f32[512]{0:T(512)S(1)}, f32[512]{0:T(512)S(1)}) all-reduce(f32[512]{0:T(512)S(1)} %get-tuple-element.26, f32[512]{0:T(512)S(1)} %get-tuple-element.25), channel_id=1, replica_groups=mesh['seq'=16,'wr'=4,'wc'=4] {'wc'}, use_global_device_ids=true, to_apply=%region_24.25 | all-reduce | flops 1024 | bytes 8192 | tf_op jit(solution)/shard_map/psum | solution.py:225
  541.4 5.2 fusion.18
  546.7 3.5 copy.268
  550.1 7.6 %all-to-all-start.5 = ((bf16[512,16,128]{2,0,1:T(8,128)(2,1)}), bf16[512,16,128]{2,0,1:T(8,128)(2,1)S(1)}, u32[]{:S(2)}, u32[]{:S(2)}) async-start(bf16[512,16,128]{2,0,1:T(8,128)(2,1)} %bitcast.287), calls=%async_computation.5 | async-start | bytes 4194304 | tf_op jit(solution)/shard_map/all_to_all | solution.py:239
  559.5 82.8 %psum.39 = bf16[2,3,3,256]{3,1,2,0:T(4,128)(2,1)S(1)} all-reduce(bf16[2,3,3,256]{3,1,2,0:T(4,128)(2,1)S(1)} %copy.221), channel_id=1, replica_groups=mesh['seq'=16,'wr'=4,'wc'=4] {'seq'}, use_global_device_ids=true, to_apply=%region_38.39 | all-reduce | flops 4608 | bytes 18432 | tf_op jit(solution)/shard_map/psum | solution.py:257
  643.1 4.1 copy.271
  648.8 2.8 copy.270
  651.5 2.6 fusion.10
  (290 shorter events, 78.5 us)
Async XLA Ops:
  7.2 56.9 %all-gather.11.cloned.1.call-start = ((), (), s32[]{:S(2)}) async-start(), calls=%async_computation.6 | async-start | bytes 2228224 | tf_op jit(solution)/shard_map/all_gather | solution.py:155
  7.9 84.8 %all-gather.15.cloned.1.call-start = ((), (), s32[]{:S(2)}) async-start(), calls=%async_computation.8 | async-start | bytes 1310720 | tf_op jit(solution)/shard_map/all_gather | solution.py:172
  12.5 63.9 %copy-start.36 = (s32[512]{0:T(512)}, s32[512]{0:T(512)S(1)}, u32[]{:S(2)}) copy-start(s32[512]{0:T(512)S(1)} %convert_add_fusion) | copy-start | bytes 6148
  68.1 12.0 %copy-start.5 = (bf16[512,2048]{1,0:T(8,128)(2,1)}, bf16[512,2048]{1,0:T(8,128)(2,1)S(1)}, u32[]{:S(2)}) copy-start(bf16[512,2048]{1,0:T(8,128)(2,1)S(1)} %fusion.2) | copy-start | bytes 6291460
  69.6 10.5 %copy-start.22 = (bf16[2,2048,8]{1,2,0:T(8,128)(2,1)S(1)}, bf16[2,2048,8]{1,2,0:T(8,128)(2,1)}, u32[]{:S(2)}) copy-start(bf16[2,2048,8]{1,2,0:T(8,128)(2,1)} %param.20) | copy-start | bytes 196612
  69.6 47.8 %all-gather.13.cloned.1.call-start = ((), (), s32[]{:S(2)}) async-start(), calls=%async_computation.7 | async-start | bytes 1310720 | tf_op jit(solution)/shard_map/all_gather | solution.py:173
  71.0 9.8 %copy-start.25 = (f32[512]{0:T(512)}, f32[512]{0:T(512)S(1)}, u32[]{:S(2)}) copy-start(f32[512]{0:T(512)S(1)} %get-tuple-element.95) | copy-start | bytes 6148
  71.0 9.8 %copy-start.27 = (f32[512]{0:T(512)}, f32[512]{0:T(512)S(1)}, u32[]{:S(2)}) copy-start(f32[512]{0:T(512)S(1)} %get-tuple-element.96) | copy-start | bytes 6148
  71.0 9.8 %copy-start.29 = (f32[512]{0:T(512)}, f32[512]{0:T(512)S(1)}, u32[]{:S(2)}) copy-start(f32[512]{0:T(512)S(1)} %get-tuple-element.97) | copy-start | bytes 6148
  72.9 5.0 collective-permute-start
  80.1 14.4 %copy-start.54 = (f32[4]{0:T(128)}, f32[4]{0:T(128)S(1)}, u32[]{:S(2)}) copy-start(f32[4]{0:T(128)S(1)} %compare_convert_fusion.6) | copy-start | bytes 52
  120.6 5.1 copy-start
  136.1 7.3 %copy-start.24 = (f32[2,1,4,4,256]{4,3,2,1,0:T(4,128)S(1)}, f32[2,1,4,4,256]{4,3,2,1,0:T(4,128)}, u32[]{:S(2)}) copy-start(f32[2,1,4,4,256]{4,3,2,1,0:T(4,128)} %param.24) | copy-start | bytes 98308
  136.1 9.0 %copy-start.71 = (u32[256]{0:T(256)S(1)}, u32[256]{0:T(256)}, u32[]{:S(2)}) copy-start(u32[256]{0:T(256)} %constant.135) | copy-start | bytes 3076
  136.1 71.3 %all-to-all-start = ((bf16[16,3,64,256]{3,2,1,0:T(8,128)(2,1)}), bf16[16,3,64,256]{3,2,1,0:T(8,128)(2,1)}, u32[]{:S(2)}, u32[]{:S(2)}) async-start(bf16[16,3,64,256]{3,2,1,0:T(8,128)(2,1)} %pad_maximum_fusion.6), calls=%async_computation | async-start | bytes 3145728 | tf_op jit(solution)/shard_map/all_to_all | solution.py:211
  147.0 60.4 %copy-start.50 = (s32[17]{0:T(128)}, s32[17]{0:T(128)S(1)}, u32[]{:S(2)}) copy-start(s32[17]{0:T(128)S(1)} %fusion.170) | copy-start | bytes 208
  147.7 59.7 %copy-start.52 = (s32[16]{0:T(128)}, s32[16]{0:T(128)S(1)}, u32[]{:S(2)}) copy-start(s32[16]{0:T(128)S(1)} %fusion.169) | copy-start | bytes 196
  147.7 59.5 %copy-start.31 = (pred[17,16]{0,1:T(8,128)(4,1)}, pred[17,16]{0,1:T(8,128)(4,1)S(1)}, u32[]{:S(2)}) copy-start(pred[17,16]{0,1:T(8,128)(4,1)S(1)} %iota_compare_fusion.2) | copy-start | bytes 820
  147.7 59.5 %copy-start.32 = (pred[16,16]{1,0:T(8,128)(4,1)}, pred[16,16]{1,0:T(8,128)(4,1)S(1)}, u32[]{:S(2)}) copy-start(pred[16,16]{1,0:T(8,128)(4,1)S(1)} %iota_compare_fusion.1) | copy-start | bytes 772
  209.3 11.1 %copy-start.60 = (f32[2,256]{1,0:T(2,128)S(1)}, f32[2,256]{1,0:T(2,128)}, u32[]{:S(2)}) copy-start(f32[2,256]{1,0:T(2,128)} %param.27) | copy-start | bytes 6148
  209.3 11.7 %copy-start.61 = (f32[2,256]{1,0:T(2,128)S(1)}, f32[2,256]{1,0:T(2,128)}, u32[]{:S(2)}) copy-start(f32[2,256]{1,0:T(2,128)} %param.28) | copy-start | bytes 6148
  213.5 20.2 %all-to-all-start.1 = ((bf16[16,64,256]{2,1,0:T(8,128)(2,1)}), bf16[16,64,256]{2,1,0:T(8,128)(2,1)}, u32[]{:S(2)}, u32[]{:S(2)}) async-start(bf16[16,64,256]{2,1,0:T(8,128)(2,1)} %multiply_reduce_fusion.1), calls=%async_computation.1 | async-start | bytes 1048576 | tf_op jit(solution)/shard_map/all_to_all | solution.py:214
  220.3 112.6 %all-gather.17.cloned.1.call-start = ((), (), s32[]{:S(2)}) async-start(), calls=%async_computation.9 | async-start | bytes 2228224 | tf_op jit(solution)/shard_map/all_gather | solution.py:155
  221.5 5.4 copy-start.37
  221.5 5.4 copy-start.49
  226.9 6.9 %copy-start.65 = (f32[512]{0:T(512)S(1)}, f32[512]{0:T(512)}, u32[]{:S(2)}) copy-start(f32[512]{0:T(512)} %get-tuple-element.57) | copy-start | bytes 6148
  230.5 13.3 %copy-start.20 = (bf16[512,256]{1,0:T(8,128)(2,1)S(1)}, bf16[512,256]{1,0:T(8,128)(2,1)}, u32[]{:S(2)}) copy-start(bf16[512,256]{1,0:T(8,128)(2,1)} %multiply_convert_fusion.5) | copy-start | bytes 786436
  286.2 75.7 %all-gather.21.cloned.1.call-start = ((), (), s32[]{:S(2)}) async-start(), calls=%async_computation.11 | async-start | bytes 1310720 | tf_op jit(solution)/shard_map/all_gather | solution.py:172
  337.4 7.0 %copy-start.26 = (f32[512]{0:T(512)S(1)}, f32[512]{0:T(512)}, u32[]{:S(2)}) copy-start(f32[512]{0:T(512)} %copy-done.25) | copy-start | bytes 6148
  337.4 7.0 %copy-start.28 = (f32[512]{0:T(512)S(1)}, f32[512]{0:T(512)}, u32[]{:S(2)}) copy-start(f32[512]{0:T(512)} %copy-done.27) | copy-start | bytes 6148
  337.4 7.0 %copy-start.30 = (f32[512]{0:T(512)S(1)}, f32[512]{0:T(512)}, u32[]{:S(2)}) copy-start(f32[512]{0:T(512)} %copy-done.29) | copy-start | bytes 6148
  337.4 7.0 %copy-start.41 = (f32[1,1,256]{2,1,0:T(1,128)S(1)}, f32[1,1,256]{2,1,0:T(1,128)}, u32[]{:S(2)}) copy-start(f32[1,1,256]{2,1,0:T(1,128)} %get-tuple-element.80) | copy-start | bytes 3076
  337.4 7.0 %copy-start.42 = (f32[1,1,256]{2,1,0:T(1,128)S(1)}, f32[1,1,256]{2,1,0:T(1,128)}, u32[]{:S(2)}) copy-start(f32[1,1,256]{2,1,0:T(1,128)} %get-tuple-element.81) | copy-start | bytes 3076
  337.4 7.0 %copy-start.43 = (f32[1,1,256]{2,1,0:T(1,128)S(1)}, f32[1,1,256]{2,1,0:T(1,128)}, u32[]{:S(2)}) copy-start(f32[1,1,256]{2,1,0:T(1,128)} %get-tuple-element.86) | copy-start | bytes 3076
  337.4 7.0 %copy-start.44 = (f32[1,1,256]{2,1,0:T(1,128)S(1)}, f32[1,1,256]{2,1,0:T(1,128)}, u32[]{:S(2)}) copy-start(f32[1,1,256]{2,1,0:T(1,128)} %get-tuple-element.87) | copy-start | bytes 3076
  337.4 7.0 %copy-start.45 = (f32[1,256]{1,0:T(1,128)S(1)}, f32[1,256]{1,0:T(1,128)}, u32[]{:S(2)}) copy-start(f32[1,256]{1,0:T(1,128)} %get-tuple-element.108) | copy-start | bytes 3076
  338.9 7.5 %copy-start.33 = (f32[1,1,4,1,256]{4,3,2,1,0:T(1,128)S(1)}, f32[1,1,4,1,256]{4,3,2,1,0:T(1,128)}, u32[]{:S(2)}) copy-start(f32[1,1,4,1,256]{4,3,2,1,0:T(1,128)} %get-tuple-element.78) | copy-start | bytes 12292
  338.9 47.6 %all-gather.19.cloned.1.call-start = ((), (), s32[]{:S(2)}) async-start(), calls=%async_computation.10 | async-start | bytes 1310720 | tf_op jit(solution)/shard_map/all_gather | solution.py:173
  339.6 3.8 collective-permute-start.1
  345.6 4.7 copy-start.46
  345.6 6.0 copy-start.56
  345.6 6.0 copy-start.57
  345.6 6.0 copy-start.58
  350.9 38.2 %copy-start.34 = (f32[512]{0:T(512)}, f32[512]{0:T(512)S(1)}, u32[]{:S(2)}) copy-start(f32[512]{0:T(512)S(1)} %get-tuple-element.54) | copy-start | bytes 6148
  421.7 9.3 %copy-start.63 = (f32[16]{0:T(128)S(1)}, f32[16]{0:T(128)}, u32[]{:S(2)}) copy-start(f32[16]{0:T(128)} %get-tuple-element.33) | copy-start | bytes 196
  421.7 9.3 %copy-start.64 = (f32[16]{0:T(128)S(1)}, f32[16]{0:T(128)}, u32[]{:S(2)}) copy-start(f32[16]{0:T(128)} %get-tuple-element.34) | copy-start | bytes 196
  421.7 81.6 %all-to-all-start.3 = ((bf16[16,3,64,256]{3,2,1,0:T(8,128)(2,1)}), bf16[16,3,64,256]{3,2,1,0:T(8,128)(2,1)}, u32[]{:S(2)}, u32[]{:S(2)}) async-start(bf16[16,3,64,256]{3,2,1,0:T(8,128)(2,1)} %pad_maximum_fusion.7), calls=%async_computation.3 | async-start | bytes 3145728 | tf_op jit(solution)/shard_map/all_to_all | solution.py:211
  429.0 214.1 %all-gather.23.cloned.1.call-start = ((), (), s32[]{:S(2)}) async-start(), calls=%async_computation.12 | async-start | bytes 1671168 | tf_op jit(solution)/shard_map/all_gather | solution.py:220
  431.7 69.2 %copy-start.51 = (s32[17]{0:T(128)S(1)}, s32[17]{0:T(128)}, u32[]{:S(2)}) copy-start(s32[17]{0:T(128)} %copy-done.50) | copy-start | bytes 208
  431.7 69.2 %copy-start.53 = (s32[16]{0:T(128)S(1)}, s32[16]{0:T(128)}, u32[]{:S(2)}) copy-start(s32[16]{0:T(128)} %copy-done.52) | copy-start | bytes 196
  509.3 22.6 %all-to-all-start.4 = ((bf16[16,64,256]{2,1,0:T(8,128)(2,1)}), bf16[16,64,256]{2,1,0:T(8,128)(2,1)}, u32[]{:S(2)}, u32[]{:S(2)}) async-start(bf16[16,64,256]{2,1,0:T(8,128)(2,1)} %multiply_reduce_fusion), calls=%async_computation.4 | async-start | bytes 1048576 | tf_op jit(solution)/shard_map/all_to_all | solution.py:214
  516.0 5.5 copy-start.35
  516.0 5.5 copy-start.38
  516.1 5.5 copy-start.48
  516.1 132.7 %all-gather.25.cloned.1.call-start = ((), (), s32[]{:S(2)}) async-start(), calls=%async_computation.13 | async-start | bytes 1671168 | tf_op jit(solution)/shard_map/all_gather | solution.py:220
  525.1 6.8 %copy-start.47 = (f32[512]{0:T(512)S(1)}, f32[512]{0:T(512)}, u32[]{:S(2)}) copy-start(f32[512]{0:T(512)} %get-tuple-element.53) | copy-start | bytes 6148
  526.9 14.6 %copy-start.4 = (bf16[512,2048]{1,0:T(8,128)(2,1)S(1)}, bf16[512,2048]{1,0:T(8,128)(2,1)}, u32[]{:S(2)}) copy-start(bf16[512,2048]{1,0:T(8,128)(2,1)} %copy-done.3) | copy-start | bytes 6291460
  526.9 14.6 %copy-start.19 = (bf16[512,256]{1,0:T(8,128)(2,1)S(1)}, bf16[512,256]{1,0:T(8,128)(2,1)}, u32[]{:S(2)}) copy-start(bf16[512,256]{1,0:T(8,128)(2,1)} %multiply_convert_fusion.3) | copy-start | bytes 786436
  526.9 14.5 %copy-start.66 = (f32[1,256]{1,0:T(1,128)S(1)}, f32[1,256]{1,0:T(1,128)}, u32[]{:S(2)}) copy-start(f32[1,256]{1,0:T(1,128)} %get-tuple-element.102) | copy-start | bytes 3076
  526.9 14.5 %copy-start.67 = (f32[1,256]{1,0:T(1,128)S(1)}, f32[1,256]{1,0:T(1,128)}, u32[]{:S(2)}) copy-start(f32[1,256]{1,0:T(1,128)} %get-tuple-element.100) | copy-start | bytes 3076
  550.1 8.9 %copy-start.8 = (bf16[512,256]{1,0:T(8,128)(2,1)S(1)}, bf16[512,256]{1,0:T(8,128)(2,1)}, u32[]{:S(2)}) copy-start(bf16[512,256]{1,0:T(8,128)(2,1)} %convolution_convert_fusion.11) | copy-start | bytes 786436
  550.1 9.2 %copy-start.9 = (bf16[512,256]{1,0:T(8,128)(2,1)S(1)}, bf16[512,256]{1,0:T(8,128)(2,1)}, u32[]{:S(2)}) copy-start(bf16[512,256]{1,0:T(8,128)(2,1)} %convolution_convert_fusion.10) | copy-start | bytes 786436
  550.1 92.2 %copy-start.70 = (s32[2]{0:T(128)S(1)}, s32[2]{0:T(128)}, u32[]{:S(2)}) copy-start(s32[2]{0:T(128)} %param.31) | copy-start | bytes 28
  550.1 97.0 %all-to-all-start.5 = ((bf16[512,16,128]{2,0,1:T(8,128)(2,1)}), bf16[512,16,128]{2,0,1:T(8,128)(2,1)S(1)}, u32[]{:S(2)}, u32[]{:S(2)}) async-start(bf16[512,16,128]{2,0,1:T(8,128)(2,1)} %bitcast.287), calls=%async_computation.5 | async-start | bytes 4194304 | tf_op jit(solution)/shard_map/all_to_all | solution.py:239
  (23 other events, 46.9 us)
Sparse Core Ops, SparseCore 0:
  10.6 53.4 all-gather.10
  69.7 22.9 all-gather.14
  94.5 22.8 all-gather.12
  286.4 46.4 all-gather.16
  339.0 22.8 all-gather.20
  363.6 22.8 all-gather.18
  499.3 73.2 all-gather.22
  574.4 70.3 all-gather.24
